TPU v7x, 32 devices: a whole 2x2x4 slice. The times are simulated.
32 devices in a mesh: segment: 2 (over x), dp: 16 (over z, y, core).
Axes of the slice: x: 2, y: 2, z: 4, core: 2. Of those that a mesh axis runs over, the one named last changes fastest.
Arguments:
- fine_inflow: bfloat16 [2, 16, 16, 16, 256], P('segment', 'dp'), may hold values from -250 to 250
- coarse_inflow: bfloat16 [2, 16, 8, 8, 512], P('segment', 'dp'), may hold values from -250 to 250
- fine_entries: bfloat16 [3, 16, 16, 16, 256], P(None, 'dp'), may hold values from -250 to 250
- fine_pending: bfloat16 [2, 2, 16, 16, 16, 256], P('segment', None, 'dp'), may hold values from -250 to 250, as said below
- coarse_pending: bfloat16 [2, 1, 16, 8, 8, 512], P('segment', None, 'dp'), may hold values from -250 to 250, as said below
- fine_kernels: bfloat16 [2, 2, 3, 3, 256, 256], P('segment'), may hold values from -0.125 to 0.125
- fine_mixing: bfloat16 [2, 256, 256], P('segment'), may hold values from -0.375 to 0.375
- fine_gains: float32 [2, 2, 256], P('segment'), may hold values from 0.5 to 1.5
- fine_shifts: float32 [2, 2, 256], P('segment'), may hold values from -3 to 3
- coarse_kernel: bfloat16 [2, 3, 3, 512, 512], P('segment'), may hold values from -0.09375 to 0.09375
- coarse_mixing: bfloat16 [2, 512, 512], P('segment'), may hold values from -0.25 to 0.25
- coarse_gains: float32 [2, 512], P('segment'), may hold values from 0.5 to 1.5
- coarse_shifts: float32 [2, 512], P('segment'), may hold values from -3 to 3
- descent_kernel: bfloat16 [2, 2, 256, 512], replicated, may hold values from -0.1875 to 0.1875
- upsample_kernel: bfloat16 [512, 2, 2, 256], replicated, may hold values from -0.25 to 0.25
Outputs:
- fine_stash: bfloat16 [2, 4, 16, 16, 16, 256], P('segment', None, 'dp')
- coarse_stash: bfloat16 [2, 4, 16, 8, 8, 512], P('segment', None, 'dp')
- fine_backlog: bfloat16 [2, 2, 16, 16, 16, 256], P('segment', None, 'dp')
- coarse_backlog: bfloat16 [2, 1, 16, 8, 8, 512], P('segment', None, 'dp')
Inputs may be any that keep to these rules, and one draw needn't show every extreme that they name: `fine_pending`: at segments 1 and above only the first 1 slots are read. `coarse_pending`: at segments below 1 only the first 0 slots are read.
All inputs are finite; a program needn't handle non-finite values.
Results may differ from a plain program's by a relative error of at most 0.017.
Values may be sent and summed in bfloat16 or wider, within the bound.
A program may use at most 64 MiB of HBM per device.

v0:
```python
import jax
import jax.numpy as jnp
from jax import lax
from jax.sharding import PartitionSpec as P

EPSILON = 1e-05


def shifted(block, axis, distance):
    devices = range(lax.axis_size(axis))
    route = [(i - distance, i) for i in devices if i - distance in devices]
    return lax.ppermute(block, axis, route)


def for_sending(x):

    def short(part):
        return part.astype(jnp.bfloat16) if part.dtype == jnp.float32 else part

    return jax.tree.map(short, x)


def passed_along(x, axis, by):
    size = lax.axis_size(axis)
    return lax.ppermute(x, axis, [(i, (i + by) % size) for i in range(size)])


def convolve(images, kernel):
    return lax.conv_general_dilated(
        images,
        kernel,
        (1, 1),
        "SAME",
        dimension_numbers=("NHWC", "HWIO", "NHWC"),
        preferred_element_type=jnp.float32,
    )


def project(images, matrix):
    flat = images.reshape(-1, images.shape[-1])
    result = jnp.dot(flat, matrix, preferred_element_type=jnp.float32)
    return result.reshape(images.shape[:-1] + (matrix.shape[1],))


def descend(images, kernel):
    lowered = lax.conv_general_dilated(
        images,
        kernel,
        (2, 2),
        "VALID",
        dimension_numbers=("NHWC", "HWIO", "NHWC"),
        preferred_element_type=jnp.float32,
    )
    return lowered.astype(jnp.bfloat16)


def upsample(images, kernel):
    batches, height, breadth, coarse = images.shape
    fine_ch = kernel.shape[-1]
    spread = project(images, kernel.reshape(coarse, 4 * fine_ch))
    spread = spread.reshape(batches, height, breadth, 2, 2, fine_ch).transpose(0, 1, 3, 2, 4, 5)
    return spread.reshape(batches, 2 * height, 2 * breadth, fine_ch).astype(jnp.bfloat16)


def normalize(activations, gain_list, shift_list, dp_count):
    widths_list = [member.shape[-1] for member in activations]
    starts = [sum(widths_list[:member_index]) for member_index in range(len(widths_list))]
    inverse = jnp.concatenate(
        [
            jnp.full(
                (member.shape[-1],),
                1.0 / (dp_count * member.shape[1] * member.shape[2]),
                jnp.float32,
            )
            for member in activations
        ]
    )
    totals = jnp.concatenate([jnp.sum(member, axis=(0, 1, 2)) for member in activations])
    squares = jnp.concatenate(
        [jnp.sum(jnp.square(member), axis=(0, 1, 2)) for member in activations]
    )
    joined = lax.psum(jnp.concatenate([totals, squares]), "dp")
    centers = joined[: totals.shape[0]] * inverse
    spreads = joined[totals.shape[0] :] * inverse - jnp.square(centers)
    results = []
    for member_index, member in enumerate(activations):
        lower_edge = starts[member_index]
        upper_edge = lower_edge + widths_list[member_index]
        scaled = (member - centers[lower_edge:upper_edge]) * lax.rsqrt(
            spreads[lower_edge:upper_edge] + EPSILON
        ) * gain_list[member_index] + shift_list[member_index]
        results.append(jnp.maximum(scaled, 0.0).astype(jnp.bfloat16))
    return results


def on_device(
    fine_inflow,
    coarse_inflow,
    fine_entries,
    fine_pending,
    coarse_pending,
    fine_kernels,
    fine_mixing,
    fine_gains,
    fine_shifts,
    coarse_kernel,
    coarse_mixing,
    coarse_gains,
    coarse_shifts,
    descent_kernel,
    upsample_kernel,
):
    segment_count = lax.axis_size("segment")
    half_depth = segment_count // 2
    dp_count = lax.axis_size("dp")
    position = lax.axis_index("segment")
    is_lower = position < half_depth
    tick_count = fine_entries.shape[0] + 1
    hold_fine = fine_pending.shape[1]
    recv_fine = 3 * half_depth - hold_fine
    hold_coarse = coarse_pending.shape[1]
    recv_coarse = half_depth - hold_coarse
    fine_slots = [fine_pending[0, slot_index] for slot_index in range(hold_fine)]
    coarse_slots = [coarse_pending[0, slot_index] for slot_index in range(hold_coarse)]
    fine_now = fine_inflow[0]
    coarse_now = coarse_inflow[0]
    zero_fine = jnp.zeros_like(fine_now)
    zero_coarse = jnp.zeros_like(coarse_now)
    fine_made = []
    coarse_made = []
    fine_arrived = []
    coarse_arrived = []
    fine_store = []
    coarse_store = []
    for tick_now in range(tick_count):
        if tick_now > 0:
            fine_send, coarse_send = lax.cond(
                position == half_depth - 1,
                lambda: (
                    upsample(coarse_store[-1], upsample_kernel),
                    descend(fine_store[-1], descent_kernel),
                ),
                lambda: (fine_store[-1], coarse_store[-1]),
            )
            fine_recv = shifted(fine_send, "segment", 1)
            coarse_recv = jax.tree.map(
                lambda part, own: part.astype(own.dtype),
                passed_along(for_sending(coarse_send), "segment", 1),
                coarse_send,
            )
            fine_now = jnp.where(position == 0, fine_entries[tick_now - 1], fine_recv)
            coarse_now = coarse_recv
        fine_outgoing = (
            fine_slots[tick_now] if tick_now < hold_fine else fine_made[tick_now - hold_fine]
        )
        fine_arrived.append(shifted(fine_outgoing, "segment", half_depth))
        coarse_outgoing = (
            coarse_slots[tick_now]
            if tick_now < hold_coarse
            else coarse_made[tick_now - hold_coarse]
        )
        coarse_arrived.append(shifted(coarse_outgoing, "segment", -half_depth))
        fine_taken = (
            fine_slots[tick_now] if tick_now < recv_fine else fine_arrived[tick_now - recv_fine]
        )
        coarse_taken = (
            coarse_slots[tick_now]
            if tick_now < recv_coarse
            else coarse_arrived[tick_now - recv_coarse]
        )
        fine_input = lax.cond(
            is_lower,
            lambda: fine_now,
            lambda: (project(fine_now, fine_mixing[0]) + fine_taken.astype(jnp.float32)).astype(
                jnp.bfloat16
            ),
        )
        coarse_input = lax.cond(
            is_lower,
            lambda: (
                project(coarse_now, coarse_mixing[0]) + coarse_taken.astype(jnp.float32)
            ).astype(jnp.bfloat16),
            lambda: coarse_now,
        )
        fine_first, coarse_out = normalize(
            [convolve(fine_input, fine_kernels[0, 0]), convolve(coarse_input, coarse_kernel[0])],
            [fine_gains[0, 0], coarse_gains[0]],
            [fine_shifts[0, 0], coarse_shifts[0]],
            dp_count,
        )
        fine_out = normalize(
            [convolve(fine_first, fine_kernels[0, 1])],
            [fine_gains[0, 1]],
            [fine_shifts[0, 1]],
            dp_count,
        )[0]
        fine_made.append(
            lax.cond(
                is_lower,
                lambda: project(fine_out, fine_mixing[0]).astype(jnp.bfloat16),
                lambda: zero_fine,
            )
        )
        coarse_made.append(
            lax.cond(
                is_lower,
                lambda: zero_coarse,
                lambda: project(coarse_out, coarse_mixing[0]).astype(jnp.bfloat16),
            )
        )
        fine_store.append(fine_out)
        coarse_store.append(coarse_out)
    sender_fine = fine_slots + fine_made
    receiver_fine = fine_slots[:recv_fine] + fine_arrived
    sender_coarse = coarse_slots + coarse_made
    receiver_coarse = coarse_slots[:recv_coarse] + coarse_arrived
    fine_backlog = []
    for slot_index in range(hold_fine):
        kept_side = receiver_fine[tick_count + slot_index] if slot_index < recv_fine else zero_fine
        fine_backlog.append(jnp.where(is_lower, sender_fine[tick_count + slot_index], kept_side))
    coarse_backlog = []
    for slot_index in range(hold_coarse):
        kept_side = (
            receiver_coarse[tick_count + slot_index] if slot_index < recv_coarse else zero_coarse
        )
        coarse_backlog.append(
            jnp.where(is_lower, kept_side, sender_coarse[tick_count + slot_index])
        )
    fine_stash = jnp.stack(fine_store)[None]
    coarse_stash = jnp.stack(coarse_store)[None]
    return (
        fine_stash,
        coarse_stash,
        jnp.stack(fine_backlog)[None],
        jnp.stack(coarse_backlog)[None],
    )


def solution(mesh):
    placed = (
        P("segment", "dp", None, None, None),
        P("segment", "dp", None, None, None),
        P(None, "dp", None, None, None),
        P("segment", None, "dp", None, None, None),
        P("segment", None, "dp", None, None, None),
        P("segment", None, None, None, None, None),
        P("segment", None, None),
        P("segment", None, None),
        P("segment", None, None),
        P("segment", None, None, None, None),
        P("segment", None, None),
        P("segment", None),
        P("segment", None),
        P(),
        P(),
    )
    return jax.shard_map(
        on_device,
        mesh=mesh,
        in_specs=placed,
        out_specs=(
            P("segment", None, "dp", None, None, None),
            P("segment", None, "dp", None, None, None),
            P("segment", None, "dp", None, None, None),
            P("segment", None, "dp", None, None, None),
        ),
        check_vma=False,
    )
```

profile of v0, /device:TPU:3, one launch (start us, length us, event | category | flops | bytes accessed | tf_op | source)
XLA Modules:
  0.0 356.4 jit_solution(2921721181260113071)
XLA Ops:
  5.2 2.0 select_reduce_fusion.15
  7.5 4.6 %fusion.267 = (f32[512]{0:T(512)S(1)}, f32[512]{0:T(512)S(1)}, f32[1,8,8,512]{3,0,2,1:T(1,128)S(1)}) fusion(bf16[1,8,8,512]{3,0,2,1:T(2,128)(2,1)S(1)} %get-tuple-element.410, bf16[1,3,3,512,512]{4,3,2,1,0:T(8,128)(2,1)} %param.62), kind=kOutput, calls=%fused_computation.375 | convolution fusion | flops 253852672 | bytes 4919296 | tf_op jit(solution)/shard_map/conv_general_dilated | solution.py:29
  12.1 31.3 %psum.56 = f32[1536]{0:T(1024)S(1)} all-reduce(f32[1536]{0:T(1024)S(1)} %pad_maximum_fusion), channel_id=1, replica_groups=mesh['segment'=2,'dp'=16] {'dp'}, use_global_device_ids=true, to_apply=%region_8.0 | all-reduce | flops 1536 | bytes 12288 | tf_op jit(solution)/shard_map/psum | solution.py:82
  44.8 2.1 select_reduce_fusion.13
  46.9 33.0 %psum.57 = f32[512]{0:T(512)S(1)} all-reduce(f32[512]{0:T(512)S(1)} %pad_maximum_fusion.4), channel_id=1, replica_groups=mesh['segment'=2,'dp'=16] {'dp'}, use_global_device_ids=true, to_apply=%region_11.0 | all-reduce | flops 512 | bytes 4096 | tf_op jit(solution)/shard_map/psum | solution.py:82
  81.8 4.1 %collective-permute-start.3 = (bf16[1,8,8,512]{3,2,1,0:T(8,128)(2,1)S(1)}, bf16[1,8,8,512]{3,2,1,0:T(8,128)(2,1)S(1)}, u32[]{:S(2)}, u32[]{:S(2)}) collective-permute-start(bf16[1,8,8,512]{3,2,1,0:T(8,128)(2,1)S(1)} %get-tuple-element.239), channel_id=1, source_target_pairs={{0,16},{16,0},{1,17},{17,1},{2,18},{18,2},{3,19},{19,3},{4,20},{20... | collective-permute-start | bytes 196616 | tf_op jit(solution)/shard_map/ppermute | solution.py:25
  90.7 5.2 %fusion.266 = (f32[512]{0:T(512)}, f32[512]{0:T(512)}, f32[1,8,8,512]{3,0,2,1:T(1,128)S(1)}) fusion(bf16[1,8,8,512]{3,0,2,1:T(2,128)(2,1)S(1)} %get-tuple-element.411, bf16[1,3,3,512,512]{4,3,2,1,0:T(8,128)(2,1)} %param.62), kind=kOutput, calls=%fused_computation.374 | convolution fusion | flops 253852672 | bytes 4919296 | tf_op jit(solution)/shard_map/conv_general_dilated | solution.py:29
  99.9 2.7 select_reduce_fusion.11
  102.6 30.4 %psum.58 = f32[1536]{0:T(1024)S(1)} all-reduce(f32[1536]{0:T(1024)S(1)} %pad_maximum_fusion.1), channel_id=1, replica_groups=mesh['segment'=2,'dp'=16] {'dp'}, use_global_device_ids=true, to_apply=%region_24.25 | all-reduce | flops 1536 | bytes 12288 | tf_op jit(solution)/shard_map/psum | solution.py:82
  135.3 2.6 select_reduce_fusion.9
  138.0 29.6 %psum.59 = f32[512]{0:T(512)S(1)} all-reduce(f32[512]{0:T(512)S(1)} %pad_maximum_fusion.5), channel_id=1, replica_groups=mesh['segment'=2,'dp'=16] {'dp'}, use_global_device_ids=true, to_apply=%region_27.28 | all-reduce | flops 512 | bytes 4096 | tf_op jit(solution)/shard_map/psum | solution.py:82
  171.7 5.7 %collective-permute-start.7 = (bf16[1,8,8,512]{3,2,1,0:T(8,128)(2,1)}, bf16[1,8,8,512]{3,2,1,0:T(8,128)(2,1)}, u32[]{:S(2)}, u32[]{:S(2)}) collective-permute-start(bf16[1,8,8,512]{3,2,1,0:T(8,128)(2,1)} %get-tuple-element.241), channel_id=1, source_target_pairs={{0,16},{16,0},{1,17},{17,1},{2,18},{18,2},{3,19},{19,3},{4,20},{20... | collective-permute-start | bytes 196616 | tf_op jit(solution)/shard_map/ppermute | solution.py:25
  178.2 2.3 collective-permute-start.8
  188.0 5.2 %fusion.265 = (f32[512]{0:T(512)}, f32[512]{0:T(512)}, f32[1,8,8,512]{3,0,2,1:T(1,128)S(1)}) fusion(bf16[1,8,8,512]{3,0,2,1:T(2,128)(2,1)S(1)} %get-tuple-element.412, bf16[1,3,3,512,512]{4,3,2,1,0:T(8,128)(2,1)} %param.62), kind=kOutput, calls=%fused_computation.373 | convolution fusion | flops 253852672 | bytes 4919296 | tf_op jit(solution)/shard_map/conv_general_dilated | solution.py:29
  195.5 1.9 select_reduce_fusion.7
  198.1 31.8 %psum.60 = f32[1536]{0:T(1024)} all-reduce(f32[1536]{0:T(1024)} %pad_maximum_fusion.2), channel_id=1, replica_groups=mesh['segment'=2,'dp'=16] {'dp'}, use_global_device_ids=true, to_apply=%region_40.41 | all-reduce | flops 1536 | bytes 12288 | tf_op jit(solution)/shard_map/psum | solution.py:82
  232.6 1.9 select_reduce_fusion.5
  235.2 30.1 %psum.61 = f32[512]{0:T(512)} all-reduce(f32[512]{0:T(512)} %pad_maximum_fusion.6), channel_id=1, replica_groups=mesh['segment'=2,'dp'=16] {'dp'}, use_global_device_ids=true, to_apply=%region_43.44 | all-reduce | flops 512 | bytes 4096 | tf_op jit(solution)/shard_map/psum | solution.py:82
  268.5 7.7 %collective-permute-start.11 = (bf16[1,8,8,512]{3,2,1,0:T(8,128)(2,1)S(1)}, bf16[1,8,8,512]{3,2,1,0:T(8,128)(2,1)S(1)}, u32[]{:S(2)}, u32[]{:S(2)}) collective-permute-start(bf16[1,8,8,512]{3,2,1,0:T(8,128)(2,1)S(1)} %get-tuple-element.243), channel_id=1, source_target_pairs={{0,16},{16,0},{1,17},{17,1},{2,18},{18,2},{3,19},{19,3},{4,20},{20... | collective-permute-start | bytes 196616 | tf_op jit(solution)/shard_map/ppermute | solution.py:25
  280.7 4.6 %fusion.264 = (f32[512]{0:T(512)S(1)}, f32[512]{0:T(512)S(1)}, f32[1,8,8,512]{3,0,2,1:T(1,128)S(1)}) fusion(bf16[1,8,8,512]{3,0,2,1:T(2,128)(2,1)S(1)} %get-tuple-element.413, bf16[1,3,3,512,512]{4,3,2,1,0:T(8,128)(2,1)} %param.62), kind=kOutput, calls=%fused_computation.372 | convolution fusion | flops 253852672 | bytes 4919296 | tf_op jit(solution)/shard_map/conv_general_dilated | solution.py:29
  287.7 1.9 select_reduce_fusion.3
  289.7 31.2 %psum.62 = f32[1536]{0:T(1024)S(1)} all-reduce(f32[1536]{0:T(1024)S(1)} %pad_maximum_fusion.3), channel_id=1, replica_groups=mesh['segment'=2,'dp'=16] {'dp'}, use_global_device_ids=true, to_apply=%region_58.59 | all-reduce | flops 1536 | bytes 12288 | tf_op jit(solution)/shard_map/psum | solution.py:82
  321.4 2.0 select_reduce_fusion.1
  323.4 29.4 %psum.63 = f32[512]{0:T(512)S(1)} all-reduce(f32[512]{0:T(512)S(1)} %pad_maximum_fusion.7), channel_id=1, replica_groups=mesh['segment'=2,'dp'=16] {'dp'}, use_global_device_ids=true, to_apply=%region_61.62 | all-reduce | flops 512 | bytes 4096 | tf_op jit(solution)/shard_map/psum | solution.py:82
  (219 shorter events, 62.4 us)
Async XLA Ops:
  0.7 6.6 %collective-permute-start = (bf16[1,8,8,512]{3,2,1,0:T(8,128)(2,1)}, bf16[1,8,8,512]{3,2,1,0:T(8,128)(2,1)S(1)}, u32[]{:S(2)}, u32[]{:S(2)}) collective-permute-start(bf16[1,8,8,512]{3,2,1,0:T(8,128)(2,1)} %bitcast.488), channel_id=1, source_target_pairs={{16,0},{17,1},{18,2},{19,3},{20,4},{21,5},{22,6},{23,7},{24,8},{25... | collective-permute-start | bytes 196616 | tf_op jit(solution)/shard_map/ppermute | solution.py:12
  5.2 39.5 %copy-start.16 = (f32[1,1,256]{2,1,0:T(1,128)}, f32[1,1,256]{2,1,0:T(1,128)S(1)}, u32[]{:S(2)}) copy-start(f32[1,1,256]{2,1,0:T(1,128)S(1)} %get-tuple-element.475) | copy-start | bytes 3076
  5.2 74.8 %copy-start.10 = (f32[1,1,256]{2,1,0:T(1,128)}, f32[1,1,256]{2,1,0:T(1,128)S(1)}, u32[]{:S(2)}) copy-start(f32[1,1,256]{2,1,0:T(1,128)S(1)} %get-tuple-element.474) | copy-start | bytes 3076
  7.2 37.4 %copy-start.19 = (f32[1,1,256]{2,1,0:T(1,128)}, f32[1,1,256]{2,1,0:T(1,128)S(1)}, u32[]{:S(2)}) copy-start(f32[1,1,256]{2,1,0:T(1,128)S(1)} %get-tuple-element.473) | copy-start | bytes 3076
  7.2 72.7 %copy-start.13 = (f32[1,1,256]{2,1,0:T(1,128)}, f32[1,1,256]{2,1,0:T(1,128)S(1)}, u32[]{:S(2)}) copy-start(f32[1,1,256]{2,1,0:T(1,128)S(1)} %get-tuple-element.472) | copy-start | bytes 3076
  7.4 36.0 %copy-start.6 = (f32[768]{0:T(1024)S(1)}, f32[768]{0:T(1024)}, u32[]{:S(2)}) copy-start(f32[768]{0:T(1024)} %constant.19.clone.1) | copy-start | bytes 9220
  7.4 36.0 %copy-start.7 = (f32[768]{0:T(1024)S(1)}, f32[768]{0:T(1024)}, u32[]{:S(2)}) copy-start(f32[768]{0:T(1024)} %constant.21.clone.1) | copy-start | bytes 9220
  44.8 35.3 %copy-start.8 = (f32[1,512]{1,0:T(1,128)S(1)}, f32[1,512]{1,0:T(1,128)}, u32[]{:S(2)}) copy-start(f32[1,512]{1,0:T(1,128)} %param.65) | copy-start | bytes 6148
  44.8 35.3 %copy-start.9 = (f32[1,512]{1,0:T(1,128)S(1)}, f32[1,512]{1,0:T(1,128)}, u32[]{:S(2)}) copy-start(f32[1,512]{1,0:T(1,128)} %param.64) | copy-start | bytes 6148
  44.8 36.2 %copy-start.1 = (bf16[2,2,256,512]{3,2,1,0:T(8,128)(2,1)S(1)}, bf16[2,2,256,512]{3,2,1,0:T(8,128)(2,1)}, u32[]{:S(2)}) copy-start(bf16[2,2,256,512]{3,2,1,0:T(8,128)(2,1)} %param.66) | copy-start | bytes 3145732
  44.8 36.2 %copy-start.2 = (bf16[512,2,2,256]{3,2,1,0:T(2,128)(2,1)S(1)}, bf16[512,2,2,256]{3,2,1,0:T(2,128)(2,1)}, u32[]{:S(2)}) copy-start(bf16[512,2,2,256]{3,2,1,0:T(2,128)(2,1)} %param.67) | copy-start | bytes 3145732
  81.8 8.7 %collective-permute-start.3 = (bf16[1,8,8,512]{3,2,1,0:T(8,128)(2,1)S(1)}, bf16[1,8,8,512]{3,2,1,0:T(8,128)(2,1)S(1)}, u32[]{:S(2)}, u32[]{:S(2)}) collective-permute-start(bf16[1,8,8,512]{3,2,1,0:T(8,128)(2,1)S(1)} %get-tuple-element.239), channel_id=1, source_target_pairs={{0,16},{16,0},{1,17},{17,1},{2,18},{18,2},{3,19},{19,3},{4,20},{20... | collective-permute-start | bytes 196616 | tf_op jit(solution)/shard_map/ppermute | solution.py:25
  86.2 4.4 %collective-permute-start.4 = (bf16[1,8,8,512]{3,2,1,0:T(8,128)(2,1)S(1)}, bf16[1,8,8,512]{3,2,1,0:T(8,128)(2,1)S(1)}, u32[]{:S(2)}, u32[]{:S(2)}) collective-permute-start(bf16[1,8,8,512]{3,2,1,0:T(8,128)(2,1)S(1)} %get-tuple-element.510), channel_id=1, source_target_pairs={{16,0},{17,1},{18,2},{19,3},{20,4},{21,5},{22,6},{23,7},{24,8},{25... | collective-permute-start | bytes 196616 | tf_op jit(solution)/shard_map/ppermute | solution.py:12
  87.9 10.6 %collective-permute-start.2 = (bf16[1,16,16,256]{3,2,1,0:T(8,128)(2,1)S(1)}, bf16[1,16,16,256]{3,2,1,0:T(8,128)(2,1)}, u32[]{:S(2)}, u32[]{:S(2)}) collective-permute-start(bf16[1,16,16,256]{3,2,1,0:T(8,128)(2,1)S(1)} %get-tuple-element.439), channel_id=1, source_target_pairs={{0,16},{1,17},{2,18},{3,19},{4,20},{5,21},{6,22},{7,23},{8,24},{9,... | collective-permute-start | bytes 393224 | tf_op jit(solution)/shard_map/ppermute | solution.py:12
  89.2 8.3 %collective-permute-start.1 = (bf16[1,16,16,256]{3,2,1,0:T(8,128)(2,1)}, bf16[1,16,16,256]{3,2,1,0:T(8,128)(2,1)}, u32[]{:S(2)}, u32[]{:S(2)}) collective-permute-start(bf16[1,16,16,256]{3,2,1,0:T(8,128)(2,1)} %get-tuple-element.238), channel_id=1, source_target_pairs={{0,16},{1,17},{2,18},{3,19},{4,20},{5,21},{6,22},{7,23},{8,24},{9,... | collective-permute-start | bytes 393224 | tf_op jit(solution)/shard_map/ppermute | solution.py:12
  171.7 14.1 %collective-permute-start.7 = (bf16[1,8,8,512]{3,2,1,0:T(8,128)(2,1)}, bf16[1,8,8,512]{3,2,1,0:T(8,128)(2,1)}, u32[]{:S(2)}, u32[]{:S(2)}) collective-permute-start(bf16[1,8,8,512]{3,2,1,0:T(8,128)(2,1)} %get-tuple-element.241), channel_id=1, source_target_pairs={{0,16},{16,0},{1,17},{17,1},{2,18},{18,2},{3,19},{19,3},{4,20},{20... | collective-permute-start | bytes 196616 | tf_op jit(solution)/shard_map/ppermute | solution.py:25
  178.2 8.9 %collective-permute-start.8 = (bf16[1,8,8,512]{3,2,1,0:T(8,128)(2,1)}, bf16[1,8,8,512]{3,2,1,0:T(8,128)(2,1)}, u32[]{:S(2)}, u32[]{:S(2)}) collective-permute-start(bf16[1,8,8,512]{3,2,1,0:T(8,128)(2,1)} %get-tuple-element.512), channel_id=1, source_target_pairs={{16,0},{17,1},{18,2},{19,3},{20,4},{21,5},{22,6},{23,7},{24,8},{25... | collective-permute-start | bytes 196616 | tf_op jit(solution)/shard_map/ppermute | solution.py:12
  180.5 13.7 %collective-permute-start.6 = (bf16[1,16,16,256]{3,2,1,0:T(8,128)(2,1)}, bf16[1,16,16,256]{3,2,1,0:T(8,128)(2,1)}, u32[]{:S(2)}, u32[]{:S(2)}) collective-permute-start(bf16[1,16,16,256]{3,2,1,0:T(8,128)(2,1)} %get-tuple-element.438), channel_id=1, source_target_pairs={{0,16},{1,17},{2,18},{3,19},{4,20},{5,21},{6,22},{7,23},{8,24},{9,... | collective-permute-start | bytes 393224 | tf_op jit(solution)/shard_map/ppermute | solution.py:12
  182.5 103.9 %collective-permute-start.10 = (bf16[1,16,16,256]{3,2,1,0:T(8,128)(2,1)}, bf16[1,16,16,256]{3,2,1,0:T(8,128)(2,1)}, u32[]{:S(2)}, u32[]{:S(2)}) collective-permute-start(bf16[1,16,16,256]{3,2,1,0:T(8,128)(2,1)} %get-tuple-element.513), channel_id=1, source_target_pairs={{0,16},{1,17},{2,18},{3,19},{4,20},{5,21},{6,22},{7,23},{8,24},{9,... | collective-permute-start | bytes 393224 | tf_op jit(solution)/shard_map/ppermute | solution.py:12
  183.8 9.4 %collective-permute-start.5 = (bf16[1,16,16,256]{3,2,1,0:T(8,128)(2,1)}, bf16[1,16,16,256]{3,2,1,0:T(8,128)(2,1)S(1)}, u32[]{:S(2)}, u32[]{:S(2)}) collective-permute-start(bf16[1,16,16,256]{3,2,1,0:T(8,128)(2,1)} %get-tuple-element.240), channel_id=1, source_target_pairs={{0,16},{1,17},{2,18},{3,19},{4,20},{5,21},{6,22},{7,23},{8,24},{9,... | collective-permute-start | bytes 393224 | tf_op jit(solution)/shard_map/ppermute | solution.py:12
  185.8 92.5 %collective-permute-start.13 = (bf16[1,16,16,256]{3,2,1,0:T(8,128)(2,1)}, bf16[1,16,16,256]{3,2,1,0:T(8,128)(2,1)}, u32[]{:S(2)}, u32[]{:S(2)}) collective-permute-start(bf16[1,16,16,256]{3,2,1,0:T(8,128)(2,1)} %get-tuple-element.517), channel_id=1, source_target_pairs={{0,16},{1,17},{2,18},{3,19},{4,20},{5,21},{6,22},{7,23},{8,24},{9,... | collective-permute-start | bytes 393224 | tf_op jit(solution)/shard_map/ppermute | solution.py:12
  268.5 12.0 %collective-permute-start.11 = (bf16[1,8,8,512]{3,2,1,0:T(8,128)(2,1)S(1)}, bf16[1,8,8,512]{3,2,1,0:T(8,128)(2,1)S(1)}, u32[]{:S(2)}, u32[]{:S(2)}) collective-permute-start(bf16[1,8,8,512]{3,2,1,0:T(8,128)(2,1)S(1)} %get-tuple-element.243), channel_id=1, source_target_pairs={{0,16},{16,0},{1,17},{17,1},{2,18},{18,2},{3,19},{19,3},{4,20},{20... | collective-permute-start | bytes 196616 | tf_op jit(solution)/shard_map/ppermute | solution.py:25
  276.5 4.1 %collective-permute-start.12 = (bf16[1,8,8,512]{3,2,1,0:T(8,128)(2,1)S(1)}, bf16[1,8,8,512]{3,2,1,0:T(8,128)(2,1)S(1)}, u32[]{:S(2)}, u32[]{:S(2)}) collective-permute-start(bf16[1,8,8,512]{3,2,1,0:T(8,128)(2,1)S(1)} %get-tuple-element.515), channel_id=1, source_target_pairs={{16,0},{17,1},{18,2},{19,3},{20,4},{21,5},{22,6},{23,7},{24,8},{25... | collective-permute-start | bytes 196616 | tf_op jit(solution)/shard_map/ppermute | solution.py:12
  279.2 6.2 %collective-permute-start.9 = (bf16[1,16,16,256]{3,2,1,0:T(8,128)(2,1)}, bf16[1,16,16,256]{3,2,1,0:T(8,128)(2,1)S(1)}, u32[]{:S(2)}, u32[]{:S(2)}) collective-permute-start(bf16[1,16,16,256]{3,2,1,0:T(8,128)(2,1)} %get-tuple-element.242), channel_id=1, source_target_pairs={{0,16},{1,17},{2,18},{3,19},{4,20},{5,21},{6,22},{7,23},{8,24},{9,... | collective-permute-start | bytes 393224 | tf_op jit(solution)/shard_map/ppermute | solution.py:12
  (21 other events, 363.7 us)
where the time goes:
time: 359 us; the launch traced here: 356 us
  blocking collectives  247 us (69%)
  matrix products  42.6 us (12%)
  starting transfers between devices  33.8 us (9%)
  other arithmetic  17.7 us (5%)
  local copies, waits for them, and re-layouts  11.5 us (3%)
    psum x8, blocking collectives, normalize(): joined = lax.psum(jnp.concatenate([totals, squares]), 'dp')  247 us
    conv_general_dilated x12, matrix products, convolve(): lax.conv_general_dilated(images, kernel, (1, 1), 'SAME', dimension_number...  36.7 us
    ppermute x3, starting transfers between devices, passed_along(): return lax.ppermute(x, axis, [(i, (i + by) % size) for i in range(size)])  17.5 us
    ppermute x11, starting transfers between devices, shifted(): return lax.ppermute(block, axis, route)  16.3 us
  transfers between devices with their start and end apart: 14, of which 2 were waited for; matrix products, arithmetic and copies ran while one was open for 11% of the time, Pallas kernels for 0%

commit v1 on v0

v1 whole, which is shorter than its diff:
```python
import functools

import jax
import jax.numpy as jnp
from jax import lax
from jax.experimental import pallas as pl
from jax.experimental.pallas import tpu as pltpu
from jax.sharding import PartitionSpec as P

EPSILON = 1e-05
LANES = 128
MESH = pl.DeviceIdType.MESH
F32 = jnp.float32
BF16 = jnp.bfloat16


def dot(a, b):
    return jnp.dot(a, b, preferred_element_type=F32)


def side_shifts(x, side):
    cells = x.shape[0]
    column = lax.rem(lax.broadcasted_iota(jnp.int32, x.shape, 0), side)
    before = jnp.where(column == 0, 0.0, pltpu.roll(x, 1, 0))
    after = jnp.where(column == side - 1, 0.0, pltpu.roll(x, cells - 1, 0))
    return before, x, after


def spread_taps(x, cols, side):
    cells, width = x.shape
    edge = jnp.zeros((side, width), F32)
    for dc, part in enumerate(side_shifts(x, side)):
        above = jnp.concatenate([edge, part[: cells - side]], axis=0)
        below = jnp.concatenate([part[side:], edge], axis=0)
        for dr, moved in enumerate((above, part, below)):
            start = (3 * dr + dc) * width
            cols[:, start : start + width] = moved.astype(BF16)


def put_stats(h, out):
    width = h.shape[1]
    rows = width // LANES
    total = jnp.sum(h, axis=0, keepdims=True)
    square = jnp.sum(h * h, axis=0, keepdims=True)
    for row in range(rows):
        lanes = slice(row * LANES, (row + 1) * LANES)
        out[row : row + 1, :] = total[:, lanes]
        out[rows + row : rows + row + 1, :] = square[:, lanes]


def norm_terms(total, gain, shift, count):
    rows = total.shape[0] // 2
    sums = jnp.concatenate([total[row : row + 1] for row in range(rows)], axis=1)
    squares = jnp.concatenate([total[rows + row : rows + row + 1] for row in range(rows)], axis=1)
    center = sums * (1.0 / count)
    spread = jnp.maximum(squares * (1.0 / count) - center * center, 0.0)
    scale = lax.rsqrt(spread + EPSILON) * gain
    return scale, shift - center * scale


def kernel(
    dims,
    fine_in, coarse_in, entries, fine_pend, coarse_pend,
    wf_hbm, mixf_hbm, fgain, fshift, wc_hbm, mixc_hbm, cgain, cshift, wd_hbm, wu_hbm,
    fst_out, cst_out, fback_out, cback_out,
    wf, mixf, wc, mixc, wd, wu,
    fin, cin, upin, skf, skc, fst, cst, dbuf,
    xs, hf, hc, upscr, colf, colc, zf, zc,
    statf, statc, gotf, gotc,
    load_sem, save_sem,
    fin_r, cin_r, up_r, skf_r, skc_r,
    fin_s, cin_s, up_s, skf_s, skc_s,
    gotf_r, gotc_r, statf_s, statc_s,
):
    nseg, ndp, ticks, fside, cside, hold_f, recv_f, hold_c, recv_c = dims
    half = nseg // 2
    seg = lax.axis_index("segment")
    me = lax.axis_index("dp")
    lower = seg < half
    upper = seg >= half
    turn = seg == half - 1
    after = lax.rem(seg + 1, nseg)
    mate = lax.rem(seg + half, nseg)

    def load(k, src, dst):
        return pltpu.make_async_copy(src, dst, load_sem.at[k])

    loads = [
        load(0, fine_in, fin.at[0]),
        load(1, wf_hbm, wf),
        load(2, mixf_hbm, mixf),
        load(3, coarse_in, cin.at[0]),
        load(4, mixc_hbm, mixc),
        load(5, wc_hbm, wc),
        load(6, wd_hbm, wd),
        load(7, wu_hbm, wu),
    ]
    for item in loads:
        item.start()
    own_entries = load(8, entries, fin.at[pl.ds(1, ticks - 1)])
    fine_lower = load(9, fine_pend, skf.at[pl.ds(0, hold_f)])
    coarse_upper = load(10, coarse_pend, skc.at[pl.ds(0, hold_c)])

    @pl.when(seg == 0)
    def _():
        own_entries.start()

    @pl.when(lower)
    def _():
        fine_lower.start()
        if recv_c:
            load(10, coarse_pend.at[pl.ds(0, recv_c)], skc.at[pl.ds(0, recv_c)]).start()

    @pl.when(upper)
    def _():
        coarse_upper.start()
        if recv_f:
            load(9, fine_pend.at[pl.ds(0, recv_f)], skf.at[pl.ds(0, recv_f)]).start()

    barrier = pltpu.get_barrier_semaphore()
    offsets = sorted({1 % nseg, nseg - 1, half})

    def greet(k, carry):
        pl.semaphore_signal(
            barrier, inc=1, device_id=(seg, lax.rem(me + k, ndp)), device_id_type=MESH
        )
        return carry

    lax.fori_loop(1, ndp, greet, 0)
    for offset in offsets:
        pl.semaphore_signal(
            barrier, inc=1, device_id=(lax.rem(seg + offset, nseg), me), device_id_type=MESH
        )
    zf[...] = jnp.zeros_like(zf)
    zc[...] = jnp.zeros_like(zc)
    pl.semaphore_wait(barrier, ndp - 1 + len(offsets))

    def push(src, dst, ssem, rsem, to):
        return pltpu.make_async_remote_copy(
            src_ref=src, dst_ref=dst, send_sem=ssem, recv_sem=rsem,
            device_id=(to, me), device_id_type=MESH,
        )

    def send_skf(j):
        return push(skf.at[j], skf.at[recv_f + j], skf_s.at[j], skf_r.at[j], mate)

    def send_skc(j):
        return push(skc.at[j], skc.at[recv_c + j], skc_s.at[j], skc_r.at[j], mate)

    def send_up(t):
        return push(cst.at[t], upin.at[t], up_s.at[t], up_r.at[t], after)

    def send_co(t):
        return push(cst.at[t], cin.at[t + 1], cin_s.at[t], cin_r.at[t], after)

    def send_down(t):
        return push(dbuf.at[t], cin.at[t + 1], cin_s.at[t], cin_r.at[t], after)

    def send_fo(t):
        return push(fst.at[t], fin.at[t + 1], fin_s.at[t], fin_r.at[t], after)

    def exchange(src, dst, ssem, rsem):
        def one(k, carry):
            pltpu.make_async_remote_copy(
                src_ref=src, dst_ref=dst.at[k - 1], send_sem=ssem, recv_sem=rsem,
                device_id=(seg, lax.rem(me + k, ndp)), device_id_type=MESH,
            ).start()
            return carry

        lax.fori_loop(1, ndp, one, 0)

    def whole(dst, ssem, rsem):
        return pltpu.make_async_remote_copy(
            src_ref=dst, dst_ref=dst, send_sem=ssem, recv_sem=rsem,
            device_id=(seg, lax.rem(me + 1, ndp)), device_id_type=MESH,
        )

    @pl.when(lower)
    def _():
        fine_lower.wait()
        for j in range(min(hold_f, ticks)):
            send_skf(j).start()
        if recv_c:
            load(10, coarse_pend.at[pl.ds(0, recv_c)], skc.at[pl.ds(0, recv_c)]).wait()

    @pl.when(upper)
    def _():
        coarse_upper.wait()
        for j in range(min(hold_c, ticks)):
            send_skc(j).start()
        if recv_f:
            load(9, fine_pend.at[pl.ds(0, recv_f)], skf.at[pl.ds(0, recv_f)]).wait()

    @pl.when(seg == 0)
    def _():
        own_entries.wait()

    for item in loads:
        item.wait()

    fcount = ndp * fside * fside
    ccount = ndp * cside * cside

    def save_f(t):
        return pltpu.make_async_copy(fst.at[t], fst_out.at[t], save_sem.at[0, t])

    def save_c(t):
        return pltpu.make_async_copy(cst.at[t], cst_out.at[t], save_sem.at[1, t])

    def tick(t, carry):
        @pl.when(lower)
        def _():
            @pl.when(jnp.logical_and(seg > 0, t > 0))
            def _():
                send_fo(t - 1).wait_recv()

            xs[...] = fin[t].astype(F32)

        @pl.when(upper)
        def _():
            @pl.when(jnp.logical_and(seg == half, t > 0))
            def _():
                send_up(t - 1).wait_recv()
                spread = dot(upin[t - 1], wu[...])
                width = spread.shape[1] // 4
                for a in range(2):
                    for c in range(2):
                        start = (2 * a + c) * width
                        part = spread[:, start : start + width].reshape(cside, cside, width)
                        for i in range(width // LANES):
                            lanes = slice(i * LANES, (i + 1) * LANES)
                            upscr[i, :, pl.ds(a * fside + c, cside, stride=2), :] = part[:, :, lanes]
                for i in range(width // LANES):
                    lanes = slice(i * LANES, (i + 1) * LANES)
                    fin[t, :, lanes] = upscr[i].reshape(fside * fside, LANES).astype(BF16)

            @pl.when(jnp.logical_and(seg != half, t > 0))
            def _():
                send_fo(t - 1).wait_recv()

            @pl.when(t >= recv_f)
            def _():
                send_skf(t - recv_f).wait_recv()

            xs[...] = (dot(fin[t], mixf[...]) + skf[t].astype(F32)).astype(BF16).astype(F32)

        spread_taps(xs[...], colf, fside)
        hf[...] = dot(colf[...], wf[0])
        put_stats(hf[...], statf.at[2 * t])
        exchange(statf.at[2 * t], gotf.at[2 * t], statf_s.at[2 * t], gotf_r.at[2 * t])

        @pl.when(t > 0)
        def _():
            send_co(t - 1).wait_recv()

        @pl.when(lower)
        def _():
            @pl.when(t >= recv_c)
            def _():
                send_skc(t - recv_c).wait_recv()

            hc[...] = (dot(cin[t], mixc[...]) + skc[t].astype(F32)).astype(BF16).astype(F32)

        @pl.when(upper)
        def _():
            hc[...] = cin[t].astype(F32)

        spread_taps(hc[...], colc, cside)
        hc[...] = dot(colc[...], wc[...])
        put_stats(hc[...], statc.at[t])
        exchange(statc.at[t], gotc.at[t], statc_s.at[t], gotc_r.at[t])

        whole(gotf.at[2 * t], statf_s.at[2 * t], gotf_r.at[2 * t]).wait_recv()
        total = statf[2 * t] + jnp.sum(gotf[2 * t], axis=0)
        scale, offset = norm_terms(total, fgain[0:1, :], fshift[0:1, :], fcount)
        xs[...] = jnp.maximum(hf[...] * scale + offset, 0.0).astype(BF16).astype(F32)
        spread_taps(xs[...], colf, fside)
        hf[...] = dot(colf[...], wf[1])
        put_stats(hf[...], statf.at[2 * t + 1])
        exchange(
            statf.at[2 * t + 1], gotf.at[2 * t + 1], statf_s.at[2 * t + 1], gotf_r.at[2 * t + 1]
        )

        whole(gotc.at[t], statc_s.at[t], gotc_r.at[t]).wait_recv()
        total = statc[t] + jnp.sum(gotc[t], axis=0)
        scale, offset = norm_terms(total, cgain[...], cshift[...], ccount)
        cst[t] = jnp.maximum(hc[...] * scale + offset, 0.0).astype(BF16)

        @pl.when(t < ticks - 1)
        def _():
            @pl.when(turn)
            def _():
                send_up(t).start()

            @pl.when(jnp.logical_not(turn))
            def _():
                send_co(t).start()

        save_c(t).start()

        @pl.when(upper)
        def _():
            skc[hold_c + t] = dot(cst[t], mixc[...]).astype(BF16)

            @pl.when(hold_c + t < ticks)
            def _():
                send_skc(hold_c + t).start()

        whole(gotf.at[2 * t + 1], statf_s.at[2 * t + 1], gotf_r.at[2 * t + 1]).wait_recv()
        total = statf[2 * t + 1] + jnp.sum(gotf[2 * t + 1], axis=0)
        scale, offset = norm_terms(total, fgain[1:2, :], fshift[1:2, :], fcount)
        fst[t] = jnp.maximum(hf[...] * scale + offset, 0.0).astype(BF16)

        @pl.when(t < ticks - 1)
        def _():
            @pl.when(turn)
            def _():
                width = fst.shape[2]
                for i in range(width // LANES):
                    lanes = slice(i * LANES, (i + 1) * LANES)
                    upscr[i] = fst[t, :, lanes].astype(F32).reshape(cside, 2 * fside, LANES)
                lowered = None
                for a in range(2):
                    for c in range(2):
                        for i in range(width // LANES):
                            part = upscr[i, :, pl.ds(a * fside + c, cside, stride=2), :]
                            part = part.reshape(cside * cside, LANES).astype(BF16)
                            start = (2 * a + c) * width + i * LANES
                            term = dot(part, wd[start : start + LANES, :])
                            lowered = term if lowered is None else lowered + term
                dbuf[t] = lowered.astype(BF16)
                send_down(t).start()

            @pl.when(jnp.logical_and(jnp.logical_not(turn), seg < nseg - 1))
            def _():
                send_fo(t).start()

        save_f(t).start()

        @pl.when(lower)
        def _():
            skf[hold_f + t] = dot(fst[t], mixf[...]).astype(BF16)

            @pl.when(hold_f + t < ticks)
            def _():
                send_skf(hold_f + t).start()

        return carry

    lax.fori_loop(0, ticks, tick, 0)

    def back_f(first, src):
        return pltpu.make_async_copy(src, fback_out.at[first], save_sem.at[2, first])

    def back_c(first, src):
        return pltpu.make_async_copy(src, cback_out.at[first], save_sem.at[3, first])

    lower_backs = [back_f(j, skf.at[ticks + j]) for j in range(hold_f)]
    lower_backs += [
        back_c(j, skc.at[ticks + j] if j < recv_c else zc) for j in range(hold_c)
    ]
    upper_backs = [
        back_f(j, skf.at[ticks + j] if j < recv_f else zf) for j in range(hold_f)
    ]
    upper_backs += [back_c(j, skc.at[ticks + j]) for j in range(hold_c)]

    @pl.when(lower)
    def _():
        for j in range(max(ticks - recv_c, 0), ticks):
            send_skc(j).wait_recv()
        for item in lower_backs:
            item.start()
        for j in range(ticks):
            send_skf(j).wait_send()
        for item in lower_backs:
            item.wait()

    @pl.when(upper)
    def _():
        for j in range(max(ticks - recv_f, 0), ticks):
            send_skf(j).wait_recv()
        for item in upper_backs:
            item.start()
        for j in range(ticks):
            send_skc(j).wait_send()
        for item in upper_backs:
            item.wait()

    @pl.when(turn)
    def _():
        for t in range(ticks - 1):
            send_up(t).wait_send()

    @pl.when(jnp.logical_and(jnp.logical_not(turn), seg < nseg - 1))
    def _():
        for t in range(ticks - 1):
            send_fo(t).wait_send()

    for t in range(ticks - 1):
        send_co(t).wait_send()
    for t in range(ticks):
        whole(gotf.at[2 * t], statf_s.at[2 * t], gotf_r.at[2 * t]).wait_send()
        whole(gotf.at[2 * t + 1], statf_s.at[2 * t + 1], gotf_r.at[2 * t + 1]).wait_send()
        whole(gotc.at[t], statc_s.at[t], gotc_r.at[t]).wait_send()
        save_f(t).wait()
        save_c(t).wait()


def on_device(
    fine_inflow, coarse_inflow, fine_entries, fine_pending, coarse_pending,
    fine_kernels, fine_mixing, fine_gains, fine_shifts,
    coarse_kernel, coarse_mixing, coarse_gains, coarse_shifts,
    descent_kernel, upsample_kernel,
):
    nseg = lax.axis_size("segment")
    ndp = lax.axis_size("dp")
    half = nseg // 2
    ticks = fine_entries.shape[0] + 1
    hold_f, hold_c = fine_pending.shape[1], coarse_pending.shape[1]
    recv_f, recv_c = 3 * half - hold_f, half - hold_c
    fside, fch = fine_inflow.shape[3], fine_inflow.shape[4]
    cside, cch = coarse_inflow.shape[3], coarse_inflow.shape[4]
    fcells, ccells = fside * fside, cside * cside
    dims = (nseg, ndp, ticks, fside, cside, hold_f, recv_f, hold_c, recv_c)
    frows, crows = 2 * fch // LANES, 2 * cch // LANES
    any_spec = pl.BlockSpec(memory_space=pl.ANY)
    vmem_spec = pl.BlockSpec(memory_space=pltpu.VMEM)
    dma = pltpu.SemaphoreType.DMA
    outs = pl.pallas_call(
        functools.partial(kernel, dims),
        out_shape=(
            jax.ShapeDtypeStruct((ticks, fcells, fch), BF16),
            jax.ShapeDtypeStruct((ticks, ccells, cch), BF16),
            jax.ShapeDtypeStruct((hold_f, fcells, fch), BF16),
            jax.ShapeDtypeStruct((hold_c, ccells, cch), BF16),
        ),
        in_specs=[any_spec] * 7 + [vmem_spec] * 2 + [any_spec] * 2 + [vmem_spec] * 2 + [any_spec] * 2,
        out_specs=(any_spec,) * 4,
        scratch_shapes=[
            pltpu.VMEM((2, 9 * fch, fch), BF16),
            pltpu.VMEM((fch, fch), BF16),
            pltpu.VMEM((9 * cch, cch), BF16),
            pltpu.VMEM((cch, cch), BF16),
            pltpu.VMEM((4 * fch, cch), BF16),
            pltpu.VMEM((cch, 4 * fch), BF16),
            pltpu.VMEM((ticks, fcells, fch), BF16),
            pltpu.VMEM((ticks, ccells, cch), BF16),
            pltpu.VMEM((ticks, ccells, cch), BF16),
            pltpu.VMEM((max(hold_f, recv_f) + ticks, fcells, fch), BF16),
            pltpu.VMEM((max(hold_c, recv_c) + ticks, ccells, cch), BF16),
            pltpu.VMEM((ticks, fcells, fch), BF16),
            pltpu.VMEM((ticks, ccells, cch), BF16),
            pltpu.VMEM((ticks, ccells, cch), BF16),
            pltpu.VMEM((fcells, fch), F32),
            pltpu.VMEM((fcells, fch), F32),
            pltpu.VMEM((ccells, cch), F32),
            pltpu.VMEM((fch // LANES, cside, 2 * fside, LANES), F32),
            pltpu.VMEM((fcells, 9 * fch), BF16),
            pltpu.VMEM((ccells, 9 * cch), BF16),
            pltpu.VMEM((fcells, fch), BF16),
            pltpu.VMEM((ccells, cch), BF16),
            pltpu.VMEM((2 * ticks, frows, LANES), F32),
            pltpu.VMEM((ticks, crows, LANES), F32),
            pltpu.VMEM((2 * ticks, ndp - 1, frows, LANES), F32),
            pltpu.VMEM((ticks, ndp - 1, crows, LANES), F32),
            dma((11,)),
            dma((4, max(ticks, hold_f, hold_c))),
            dma((ticks,)), dma((ticks,)), dma((ticks,)), dma((ticks,)), dma((ticks,)),
            dma((ticks,)), dma((ticks,)), dma((ticks,)), dma((ticks,)), dma((ticks,)),
            dma((2 * ticks,)), dma((ticks,)), dma((2 * ticks,)), dma((ticks,)),
        ],
        compiler_params=pltpu.CompilerParams(
            collective_id=0, has_side_effects=True, vmem_limit_bytes=56 << 20
        ),
    )(
        fine_inflow.reshape(fcells, fch),
        coarse_inflow.reshape(ccells, cch),
        fine_entries.reshape(ticks - 1, fcells, fch),
        fine_pending.reshape(hold_f, fcells, fch),
        coarse_pending.reshape(hold_c, ccells, cch),
        fine_kernels.reshape(2, 9 * fch, fch),
        fine_mixing.reshape(fch, fch),
        fine_gains.reshape(2, fch),
        fine_shifts.reshape(2, fch),
        coarse_kernel.reshape(9 * cch, cch),
        coarse_mixing.reshape(cch, cch),
        coarse_gains.reshape(1, cch),
        coarse_shifts.reshape(1, cch),
        descent_kernel.reshape(4 * fch, cch),
        upsample_kernel.reshape(cch, 4 * fch),
    )
    fst, cst, fback, cback = outs
    return (
        fst.reshape(1, ticks, 1, fside, fside, fch),
        cst.reshape(1, ticks, 1, cside, cside, cch),
        fback.reshape(1, hold_f, 1, fside, fside, fch),
        cback.reshape(1, hold_c, 1, cside, cside, cch),
    )


def solution(mesh):
    placed = (
        P("segment", "dp", None, None, None),
        P("segment", "dp", None, None, None),
        P(None, "dp", None, None, None),
        P("segment", None, "dp", None, None, None),
        P("segment", None, "dp", None, None, None),
        P("segment", None, None, None, None, None),
        P("segment", None, None),
        P("segment", None, None),
        P("segment", None, None),
        P("segment", None, None, None, None),
        P("segment", None, None),
        P("segment", None),
        P("segment", None),
        P(),
        P(),
    )
    return jax.shard_map(
        on_device,
        mesh=mesh,
        in_specs=placed,
        out_specs=(
            P("segment", None, "dp", None, None, None),
            P("segment", None, "dp", None, None, None),
            P("segment", None, "dp", None, None, None),
            P("segment", None, "dp", None, None, None),
        ),
        check_vma=False,
    )
```

time: 359 us -> 61.5 us (0.17)
  blocking collectives: 247 us -> 0 us
  Pallas kernels: 0 us -> 51.3 us
  matrix products: 42.6 us -> 0 us
  starting transfers between devices: 33.8 us -> 0 us
  other arithmetic: 17.7 us -> 0 us
    psum x8 -> x0, blocking collectives: 247 us -> none  [normalize(): joined = lax.psum(jnp.concatenate([totals, squares]), 'dp')]
    pallas_call x0 -> x1, Pallas kernels: none -> 51.3 us  [on_device(): pl.pallas_call(functools.partial(kernel, dims), out_shape=(jax.ShapeDtype...]
    conv_general_dilated x12 -> x0, matrix products: 36.7 us -> none  [convolve(): lax.conv_general_dilated(images, kernel, (1, 1), 'SAME', dimension_number...]
    ppermute x14 -> x0, starting transfers between devices: 33.8 us -> none  [the longest x3 17.5 us: passed_along(): return lax.ppermute(x, axis, [(i, (i + by) % size) for i in range(size)])]
    convert_element_type x12 -> x0, other arithmetic: 7.08 us -> none  [normalize(): results.append(jnp.maximum(scaled, 0.0).astype(jnp.bfloat16))]
    dot_general x8 -> x0, matrix products: 5.86 us -> none  [project(): result = jnp.dot(flat, matrix, preferred_element_type=jnp.float32)]
    unnamed x67 -> x4, local copies, waits for them, and re-layouts: 1.17 us -> 6.68 us
  transfers between devices with their start and end apart: 14 -> 0, of which waited for: 2 -> 0; matrix products, arithmetic and copies ran while one was open for 11% -> 0% of each run, Pallas kernels for 0% -> 0%
where the time goes in v1:
time: 61.5 us; the launch traced here: 61.2 us
  Pallas kernels  51.3 us (83%)
  local copies, waits for them, and re-layouts  9.27 us (15%)
  between operations  0.64 us (1%)
    pallas_call x1, Pallas kernels, on_device(): pl.pallas_call(functools.partial(kernel, dims), out_shape=(jax.ShapeDtype...  51.3 us
    unnamed x4, local copies, waits for them, and re-layouts  6.68 us
    reshape x1, local copies, waits for them, and re-layouts, on_device(): upsample_kernel.reshape(cch, 4 * fch)  2.59 us

profile of v1, /device:TPU:3, one launch (start us, length us, event | category | flops | bytes accessed | tf_op | source)
XLA Modules:
  0.0 61.2 jit_solution(13158886741630623403)
XLA Ops:
  0.6 2.6 %reshape.71.wu_hbm = bf16[512,1024]{1,0:T(8,128)(2,1)} reshape(bf16[512,2,2,256]{3,2,1,0:T(2,128)(2,1)} %param.29) | data formatting | bytes 2097152 | tf_op jit(solution)/shard_map/reshape | solution.py:490
  3.2 51.3 %shard_map.174 = (bf16[4,256,256]{2,1,0:T(8,128)(2,1)}, bf16[4,64,512]{2,1,0:T(8,128)(2,1)}, bf16[2,256,256]{2,1,0:T(8,128)(2,1)}, bf16[1,64,512]{2,1,0:T(8,128)(2,1)}) custom-call(bf16[256,256]{1,0:T(8,128)(2,1)} %bitcast.31, bf16[64,512]{1,0:T(8,128)(2,1)} %bitcast.33, bf16[3,256,256]{2,1,0:T(8,128)(2,1)} %bitcast.27, bf16[2,256,256]{2,1,0:T(8,128)(2,1)} %bitcast.28, ...), custom_call_target="tpu_custom_call" | custom-call | tf_op jit(solution)/shard_map/pallas_call | solution.py:429
  54.5 1.9 %copy.26 = bf16[1,4,1,16,16,256]{5,4,3,2,1,0:T(8,128)(2,1)} copy(bf16[1,4,1,16,16,256]{5,4,3,2,1,0:T(8,128)(2,1)} %bitcast.26) | data formatting | bytes 1048576
  56.4 1.7 %copy.27 = bf16[1,4,1,8,8,512]{5,4,3,2,1,0:T(8,128)(2,1)} copy(bf16[1,4,1,8,8,512]{5,4,3,2,1,0:T(8,128)(2,1)} %bitcast.30) | data formatting | bytes 524288
  58.1 1.7 %copy.28 = bf16[1,2,1,16,16,256]{5,4,3,2,1,0:T(8,128)(2,1)} copy(bf16[1,2,1,16,16,256]{5,4,3,2,1,0:T(8,128)(2,1)} %bitcast.29) | data formatting | bytes 524288
  59.7 1.5 %copy.29 = bf16[1,1,1,8,8,512]{5,4,3,2,1,0:T(8,128)(2,1)} copy(bf16[1,1,1,8,8,512]{5,4,3,2,1,0:T(8,128)(2,1)} %bitcast.35) | data formatting | bytes 131072

commit v2 on v1

--- a/solution.py
+++ b/solution.py
@@ -67,7 +67,7 @@
     fin, cin, upin, skf, skc, fst, cst, dbuf,
     xs, hf, hc, upscr, colf, colc, zf, zc,
     statf, statc, gotf, gotc,
-    load_sem, save_sem,
+    wu4, wuf, load_sem, save_sem,
     fin_r, cin_r, up_r, skf_r, skc_r,
     fin_s, cin_s, up_s, skf_s, skc_s,
     gotf_r, gotc_r, statf_s, statc_s,
@@ -85,37 +85,21 @@
     def load(k, src, dst):
         return pltpu.make_async_copy(src, dst, load_sem.at[k])
 
-    loads = [
-        load(0, fine_in, fin.at[0]),
-        load(1, wf_hbm, wf),
-        load(2, mixf_hbm, mixf),
-        load(3, coarse_in, cin.at[0]),
-        load(4, mixc_hbm, mixc),
-        load(5, wc_hbm, wc),
-        load(6, wd_hbm, wd),
-        load(7, wu_hbm, wu),
-    ]
-    for item in loads:
-        item.start()
+    get_fine = load(0, fine_in, fin.at[0])
+    get_wf0 = load(1, wf_hbm.at[0], wf.at[0])
+    get_mixf = load(2, mixf_hbm, mixf)
+    get_coarse = load(3, coarse_in, cin.at[0])
+    get_mixc = load(4, mixc_hbm, mixc)
+    get_wc = load(5, wc_hbm, wc)
+    get_wf1 = load(6, wf_hbm.at[1], wf.at[1])
+    get_wd = load(7, wd_hbm, wd)
+    get_wu = load(11, wu_hbm, wu4)
     own_entries = load(8, entries, fin.at[pl.ds(1, ticks - 1)])
-    fine_lower = load(9, fine_pend, skf.at[pl.ds(0, hold_f)])
-    coarse_upper = load(10, coarse_pend, skc.at[pl.ds(0, hold_c)])
-
-    @pl.when(seg == 0)
-    def _():
-        own_entries.start()
-
-    @pl.when(lower)
-    def _():
-        fine_lower.start()
-        if recv_c:
-            load(10, coarse_pend.at[pl.ds(0, recv_c)], skc.at[pl.ds(0, recv_c)]).start()
-
-    @pl.when(upper)
-    def _():
-        coarse_upper.start()
-        if recv_f:
-            load(9, fine_pend.at[pl.ds(0, recv_f)], skf.at[pl.ds(0, recv_f)]).start()
+    own_fine = hold_f if hold_f > ticks else 0
+    own_coarse = hold_c if hold_c > ticks else 0
+
+    def own_pend(k, src, dst, count):
+        return load(k, src.at[pl.ds(0, count)], dst.at[pl.ds(0, count)])
 
     barrier = pltpu.get_barrier_semaphore()
     offsets = sorted({1 % nseg, nseg - 1, half})
@@ -131,6 +115,38 @@
         pl.semaphore_signal(
             barrier, inc=1, device_id=(lax.rem(seg + offset, nseg), me), device_id_type=MESH
         )
+    @pl.when(upper)
+    def _():
+        if recv_f:
+            own_pend(9, fine_pend, skf, recv_f).start()
+
+    for item in (get_fine, get_wf0, get_mixf, get_coarse, get_mixc, get_wc, get_wf1):
+        item.start()
+
+    @pl.when(lower)
+    def _():
+        if recv_c:
+            own_pend(10, coarse_pend, skc, recv_c).start()
+        if own_fine:
+            own_pend(9, fine_pend, skf, own_fine).start()
+
+    @pl.when(upper)
+    def _():
+        if own_coarse:
+            own_pend(10, coarse_pend, skc, own_coarse).start()
+
+    @pl.when(seg == 0)
+    def _():
+        own_entries.start()
+
+    @pl.when(turn)
+    def _():
+        get_wd.start()
+
+    @pl.when(seg == half)
+    def _():
+        get_wu.start()
+
     zf[...] = jnp.zeros_like(zf)
     zc[...] = jnp.zeros_like(zc)
     pl.semaphore_wait(barrier, ndp - 1 + len(offsets))
@@ -143,6 +159,12 @@
 
     def send_skf(j):
         return push(skf.at[j], skf.at[recv_f + j], skf_s.at[j], skf_r.at[j], mate)
+
+    def send_pend_f(j):
+        return push(fine_pend.at[j], skf.at[recv_f + j], skf_s.at[j], skf_r.at[j], mate)
+
+    def send_pend_c(j):
+        return push(coarse_pend.at[j], skc.at[recv_c + j], skc_s.at[j], skc_r.at[j], mate)
 
     def send_skc(j):
         return push(skc.at[j], skc.at[recv_c + j], skc_s.at[j], skc_r.at[j], mate)
@@ -177,26 +199,13 @@
 
     @pl.when(lower)
     def _():
-        fine_lower.wait()
         for j in range(min(hold_f, ticks)):
-            send_skf(j).start()
-        if recv_c:
-            load(10, coarse_pend.at[pl.ds(0, recv_c)], skc.at[pl.ds(0, recv_c)]).wait()
+            send_pend_f(j).start()
 
     @pl.when(upper)
     def _():
-        coarse_upper.wait()
         for j in range(min(hold_c, ticks)):
-            send_skc(j).start()
-        if recv_f:
-            load(9, fine_pend.at[pl.ds(0, recv_f)], skf.at[pl.ds(0, recv_f)]).wait()
-
-    @pl.when(seg == 0)
-    def _():
-        own_entries.wait()
-
-    for item in loads:
-        item.wait()
+            send_pend_c(j).start()
 
     fcount = ndp * fside * fside
     ccount = ndp * cside * cside
@@ -207,7 +216,15 @@
     def save_c(t):
         return pltpu.make_async_copy(cst.at[t], cst_out.at[t], save_sem.at[1, t])
 
+    def first(t, *items):
+        @pl.when(t == 0)
+        def _():
+            for item in items:
+                item.wait()
+
     def tick(t, carry):
+        first(t, get_fine, get_mixf)
+
         @pl.when(lower)
         def _():
             @pl.when(jnp.logical_and(seg > 0, t > 0))
@@ -238,6 +255,9 @@
             def _():
                 send_fo(t - 1).wait_recv()
 
+            if recv_f:
+                first(t, own_pend(9, fine_pend, skf, recv_f))
+
             @pl.when(t >= recv_f)
             def _():
                 send_skf(t - recv_f).wait_recv()
@@ -245,16 +265,22 @@
             xs[...] = (dot(fin[t], mixf[...]) + skf[t].astype(F32)).astype(BF16).astype(F32)
 
         spread_taps(xs[...], colf, fside)
+        first(t, get_wf0)
         hf[...] = dot(colf[...], wf[0])
         put_stats(hf[...], statf.at[2 * t])
         exchange(statf.at[2 * t], gotf.at[2 * t], statf_s.at[2 * t], gotf_r.at[2 * t])
 
+        first(t, get_coarse, get_mixc)
+
         @pl.when(t > 0)
         def _():
             send_co(t - 1).wait_recv()
 
         @pl.when(lower)
         def _():
+            if recv_c:
+                first(t, own_pend(10, coarse_pend, skc, recv_c))
+
             @pl.when(t >= recv_c)
             def _():
                 send_skc(t - recv_c).wait_recv()
@@ -266,9 +292,42 @@
             hc[...] = cin[t].astype(F32)
 
         spread_taps(hc[...], colc, cside)
+        first(t, get_wc)
         hc[...] = dot(colc[...], wc[...])
         put_stats(hc[...], statc.at[t])
         exchange(statc.at[t], gotc.at[t], statc_s.at[t], gotc_r.at[t])
+
+        @pl.when(t == 0)
+        def _():
+            get_wf1.wait()
+
+            @pl.when(turn)
+            def _():
+                get_wd.wait()
+
+            @pl.when(seg == 0)
+            def _():
+                own_entries.wait()
+
+            @pl.when(seg == half)
+            def _():
+                get_wu.wait()
+                width = wu4.shape[3]
+                depth = wuf.shape[1] // 4
+
+                def rows_of(n, carry):
+                    rows = pl.multiple_of(n * depth, depth)
+                    piece = wu4[pl.ds(rows, depth)].astype(F32).reshape(4 * depth, width)
+                    for i in range(width // LANES):
+                        wuf[i] = piece[:, i * LANES : (i + 1) * LANES]
+                    for q in range(4):
+                        for i in range(width // LANES):
+                            start = q * width + i * LANES
+                            part = wuf[i, pl.ds(q, depth, stride=4), :]
+                            wu[pl.ds(rows, depth), start : start + LANES] = part.astype(BF16)
+                    return carry
+
+                lax.fori_loop(0, wu4.shape[0] // depth, rows_of, 0)
 
         whole(gotf.at[2 * t], statf_s.at[2 * t], gotf_r.at[2 * t]).wait_recv()
         total = statf[2 * t] + jnp.sum(gotf[2 * t], axis=0)
@@ -366,6 +425,8 @@
 
     @pl.when(lower)
     def _():
+        if own_fine:
+            own_pend(9, fine_pend, skf, own_fine).wait()
         for j in range(max(ticks - recv_c, 0), ticks):
             send_skc(j).wait_recv()
         for item in lower_backs:
@@ -377,6 +438,8 @@
 
     @pl.when(upper)
     def _():
+        if own_coarse:
+            own_pend(10, coarse_pend, skc, own_coarse).wait()
         for j in range(max(ticks - recv_f, 0), ticks):
             send_skf(j).wait_recv()
         for item in upper_backs:
@@ -404,6 +467,37 @@
         whole(gotc.at[t], statc_s.at[t], gotc_r.at[t]).wait_send()
         save_f(t).wait()
         save_c(t).wait()
+
+
+def hand_over_kernel(*refs):
+    count = (len(refs) - 2) // 3
+    sources, results, held = refs[:count], refs[count : 2 * count], refs[2 * count : 3 * count]
+    in_sem, out_sem = refs[3 * count :]
+    taken, given = [], []
+    for i in range(count):
+        for j in range(held[i].shape[0]):
+            taken.append(pltpu.make_async_copy(sources[i].at[j], held[i].at[j], in_sem.at[i, j]))
+            given.append(pltpu.make_async_copy(held[i].at[j], results[i].at[j], out_sem.at[i, j]))
+    for item in taken:
+        item.start()
+    for item, other in zip(taken, given):
+        item.wait()
+        other.start()
+    for item in given:
+        item.wait()
+
+
+def hand_over(arrays):
+    most = max(array.shape[0] for array in arrays)
+    any_spec = pl.BlockSpec(memory_space=pl.ANY)
+    return pl.pallas_call(
+        hand_over_kernel,
+        out_shape=tuple(jax.ShapeDtypeStruct(a.shape, a.dtype) for a in arrays),
+        in_specs=[any_spec] * len(arrays),
+        out_specs=(any_spec,) * len(arrays),
+        scratch_shapes=[pltpu.VMEM(a.shape, a.dtype) for a in arrays]
+        + [pltpu.SemaphoreType.DMA((len(arrays), most))] * 2,
+    )(*arrays)
 
 
 def on_device(
@@ -463,7 +557,9 @@
             pltpu.VMEM((ticks, crows, LANES), F32),
             pltpu.VMEM((2 * ticks, ndp - 1, frows, LANES), F32),
             pltpu.VMEM((ticks, ndp - 1, crows, LANES), F32),
-            dma((11,)),
+            pltpu.VMEM((cch, 2, 2, fch), BF16),
+            pltpu.VMEM((fch // LANES, 256, LANES), F32),
+            dma((12,)),
             dma((4, max(ticks, hold_f, hold_c))),
             dma((ticks,)), dma((ticks,)), dma((ticks,)), dma((ticks,)), dma((ticks,)),
             dma((ticks,)), dma((ticks,)), dma((ticks,)), dma((ticks,)), dma((ticks,)),
@@ -487,9 +583,9 @@
         coarse_gains.reshape(1, cch),
         coarse_shifts.reshape(1, cch),
         descent_kernel.reshape(4 * fch, cch),
-        upsample_kernel.reshape(cch, 4 * fch),
+        upsample_kernel,
     )
-    fst, cst, fback, cback = outs
+    fst, cst, fback, cback = hand_over(outs)
     return (
         fst.reshape(1, ticks, 1, fside, fside, fch),
         cst.reshape(1, ticks, 1, cside, cside, cch),

time: 61.5 us -> 52.9 us (0.86)
  local copies, waits for them, and re-layouts: 9.27 us -> 0 us
  Pallas kernels: 51.3 us -> 52.1 us
    unnamed x4 -> x0, local copies, waits for them, and re-layouts: 6.68 us -> none
    reshape x1 -> x0, local copies, waits for them, and re-layouts: 2.59 us -> none  [on_device(): upsample_kernel.reshape(cch, 4 * fch)]
    pallas_call x0 -> x1, Pallas kernels: none -> 2.24 us  [hand_over(): pl.pallas_call(hand_over_kernel, out_shape=tuple((jax.ShapeDtypeStruct(a....]
    pallas_call x1, Pallas kernels: 51.3 us -> 49.8 us  [on_device(): pl.pallas_call(functools.partial(kernel, dims), out_shape=(jax.ShapeDtype...]
where the time goes in v2:
time: 52.9 us; the launch traced here: 52.7 us
  Pallas kernels  52.1 us (98%)
  between operations  0.65 us (1%)
    pallas_call x1, Pallas kernels, on_device(): pl.pallas_call(functools.partial(kernel, dims), out_shape=(jax.ShapeDtype...  49.8 us
    pallas_call x1, Pallas kernels, hand_over(): pl.pallas_call(hand_over_kernel, out_shape=tuple((jax.ShapeDtypeStruct(a....  2.24 us

profile of v2, /device:TPU:3, one launch (start us, length us, event | category | flops | bytes accessed | tf_op | source)
XLA Modules:
  0.0 52.7 jit_solution(16775401137091597009)
XLA Ops:
  0.6 49.8 %shard_map.174 = (bf16[4,256,256]{2,1,0:T(8,128)(2,1)}, bf16[4,64,512]{2,1,0:T(8,128)(2,1)}, bf16[2,256,256]{2,1,0:T(8,128)(2,1)}, bf16[1,64,512]{2,1,0:T(8,128)(2,1)}) custom-call(bf16[256,256]{1,0:T(8,128)(2,1)} %bitcast.28, bf16[64,512]{1,0:T(8,128)(2,1)} %bitcast.30, bf16[3,256,256]{2,1,0:T(8,128)(2,1)} %bitcast.26, bf16[2,256,256]{2,1,0:T(8,128)(2,1)} %bitcast.27, ...), custom_call_target="tpu_custom_call" | custom-call | tf_op jit(solution)/shard_map/pallas_call | solution.py:523
  50.5 2.2 %shard_map.175 = (bf16[4,256,256]{2,1,0:T(8,128)(2,1)}, bf16[4,64,512]{2,1,0:T(8,128)(2,1)}, bf16[2,256,256]{2,1,0:T(8,128)(2,1)}, bf16[1,64,512]{2,1,0:T(8,128)(2,1)}) custom-call(bf16[4,256,256]{2,1,0:T(8,128)(2,1)} %get-tuple-element.12.refs_0_, bf16[4,64,512]{2,1,0:T(8,128)(2,1)} %get-tuple-element.13.refs_1_, ...), custom_call_target="tpu_custom_call" | custom-call | tf_op jit(solution)/shard_map/pallas_call | solution.py:493

commit v3 on v2

--- a/solution.py
+++ b/solution.py
@@ -65,7 +65,7 @@
     fst_out, cst_out, fback_out, cback_out,
     wf, mixf, wc, mixc, wd, wu,
     fin, cin, upin, skf, skc, fst, cst, dbuf,
-    xs, hf, hc, upscr, colf, colc, zf, zc,
+    xs, hf, hg, hc, upscr, colf, colc, zf, zc,
     statf, statc, gotf, gotc,
     wu4, wuf, load_sem, save_sem,
     fin_r, cin_r, up_r, skf_r, skc_r,
@@ -222,7 +222,7 @@
             for item in items:
                 item.wait()
 
-    def tick(t, carry):
+    def front(t):
         first(t, get_fine, get_mixf)
 
         @pl.when(lower)
@@ -270,33 +270,12 @@
         put_stats(hf[...], statf.at[2 * t])
         exchange(statf.at[2 * t], gotf.at[2 * t], statf_s.at[2 * t], gotf_r.at[2 * t])
 
-        first(t, get_coarse, get_mixc)
-
-        @pl.when(t > 0)
-        def _():
-            send_co(t - 1).wait_recv()
-
-        @pl.when(lower)
-        def _():
-            if recv_c:
-                first(t, own_pend(10, coarse_pend, skc, recv_c))
-
-            @pl.when(t >= recv_c)
-            def _():
-                send_skc(t - recv_c).wait_recv()
-
-            hc[...] = (dot(cin[t], mixc[...]) + skc[t].astype(F32)).astype(BF16).astype(F32)
-
-        @pl.when(upper)
-        def _():
-            hc[...] = cin[t].astype(F32)
-
-        spread_taps(hc[...], colc, cside)
-        first(t, get_wc)
-        hc[...] = dot(colc[...], wc[...])
-        put_stats(hc[...], statc.at[t])
-        exchange(statc.at[t], gotc.at[t], statc_s.at[t], gotc_r.at[t])
-
+    def later(which, t):
+        @pl.when(jnp.logical_and(which, t < ticks - 1))
+        def _():
+            front(t + 1)
+
+    def own_pieces(t):
         @pl.when(t == 0)
         def _():
             get_wf1.wait()
@@ -329,13 +308,44 @@
 
                 lax.fori_loop(0, wu4.shape[0] // depth, rows_of, 0)
 
+    front(jnp.int32(0))
+    own_pieces(jnp.int32(0))
+
+    def tick(t, carry):
+        first(t, get_coarse, get_mixc)
+
+        @pl.when(t > 0)
+        def _():
+            send_co(t - 1).wait_recv()
+
+        @pl.when(lower)
+        def _():
+            if recv_c:
+                first(t, own_pend(10, coarse_pend, skc, recv_c))
+
+            @pl.when(t >= recv_c)
+            def _():
+                send_skc(t - recv_c).wait_recv()
+
+            hc[...] = (dot(cin[t], mixc[...]) + skc[t].astype(F32)).astype(BF16).astype(F32)
+
+        @pl.when(upper)
+        def _():
+            hc[...] = cin[t].astype(F32)
+
+        spread_taps(hc[...], colc, cside)
+        first(t, get_wc)
+        hc[...] = dot(colc[...], wc[...])
+        put_stats(hc[...], statc.at[t])
+        exchange(statc.at[t], gotc.at[t], statc_s.at[t], gotc_r.at[t])
+
         whole(gotf.at[2 * t], statf_s.at[2 * t], gotf_r.at[2 * t]).wait_recv()
         total = statf[2 * t] + jnp.sum(gotf[2 * t], axis=0)
         scale, offset = norm_terms(total, fgain[0:1, :], fshift[0:1, :], fcount)
         xs[...] = jnp.maximum(hf[...] * scale + offset, 0.0).astype(BF16).astype(F32)
         spread_taps(xs[...], colf, fside)
-        hf[...] = dot(colf[...], wf[1])
-        put_stats(hf[...], statf.at[2 * t + 1])
+        hg[...] = dot(colf[...], wf[1])
+        put_stats(hg[...], statf.at[2 * t + 1])
         exchange(
             statf.at[2 * t + 1], gotf.at[2 * t + 1], statf_s.at[2 * t + 1], gotf_r.at[2 * t + 1]
         )
@@ -365,10 +375,12 @@
             def _():
                 send_skc(hold_c + t).start()
 
+        later(seg == 0, t)
+
         whole(gotf.at[2 * t + 1], statf_s.at[2 * t + 1], gotf_r.at[2 * t + 1]).wait_recv()
         total = statf[2 * t + 1] + jnp.sum(gotf[2 * t + 1], axis=0)
         scale, offset = norm_terms(total, fgain[1:2, :], fshift[1:2, :], fcount)
-        fst[t] = jnp.maximum(hf[...] * scale + offset, 0.0).astype(BF16)
+        fst[t] = jnp.maximum(hg[...] * scale + offset, 0.0).astype(BF16)
 
         @pl.when(t < ticks - 1)
         def _():
@@ -404,6 +416,7 @@
             def _():
                 send_skf(hold_f + t).start()
 
+        later(seg > 0, t)
         return carry
 
     lax.fori_loop(0, ticks, tick, 0)
@@ -547,6 +560,7 @@
             pltpu.VMEM((ticks, ccells, cch), BF16),
             pltpu.VMEM((fcells, fch), F32),
             pltpu.VMEM((fcells, fch), F32),
+            pltpu.VMEM((fcells, fch), F32),
             pltpu.VMEM((ccells, cch), F32),
             pltpu.VMEM((fch // LANES, cside, 2 * fside, LANES), F32),
             pltpu.VMEM((fcells, 9 * fch), BF16),

time: 52.9 us -> 52.5 us (level)
  no operation moved by 1% of the time
where the time goes in v3:
time: 52.5 us; the launch traced here: 52.3 us
  Pallas kernels  51.7 us (98%)
  between operations  0.65 us (1%)
    pallas_call x1, Pallas kernels, on_device(): pl.pallas_call(functools.partial(kernel, dims), out_shape=(jax.ShapeDtype...  49.4 us
    pallas_call x1, Pallas kernels, hand_over(): pl.pallas_call(hand_over_kernel, out_shape=tuple((jax.ShapeDtypeStruct(a....  2.24 us

profile of v3, /device:TPU:3, one launch (start us, length us, event | category | flops | bytes accessed | tf_op | source)
XLA Modules:
  0.0 52.3 jit_solution(164337949478414832)
XLA Ops:
  0.6 49.4 %shard_map.174 = (bf16[4,256,256]{2,1,0:T(8,128)(2,1)}, bf16[4,64,512]{2,1,0:T(8,128)(2,1)}, bf16[2,256,256]{2,1,0:T(8,128)(2,1)}, bf16[1,64,512]{2,1,0:T(8,128)(2,1)}) custom-call(bf16[256,256]{1,0:T(8,128)(2,1)} %bitcast.28, bf16[64,512]{1,0:T(8,128)(2,1)} %bitcast.30, bf16[3,256,256]{2,1,0:T(8,128)(2,1)} %bitcast.26, bf16[2,256,256]{2,1,0:T(8,128)(2,1)} %bitcast.27, ...), custom_call_target="tpu_custom_call" | custom-call | tf_op jit(solution)/shard_map/pallas_call | solution.py:536
  50.1 2.2 %shard_map.175 = (bf16[4,256,256]{2,1,0:T(8,128)(2,1)}, bf16[4,64,512]{2,1,0:T(8,128)(2,1)}, bf16[2,256,256]{2,1,0:T(8,128)(2,1)}, bf16[1,64,512]{2,1,0:T(8,128)(2,1)}) custom-call(bf16[4,256,256]{2,1,0:T(8,128)(2,1)} %get-tuple-element.12.refs_0_, bf16[4,64,512]{2,1,0:T(8,128)(2,1)} %get-tuple-element.13.refs_1_, ...), custom_call_target="tpu_custom_call" | custom-call | tf_op jit(solution)/shard_map/pallas_call | solution.py:506
